TPU v7x, 256 devices: a whole 4x4x8 slice. The times are simulated.
256 devices in a mesh: grp: 2 (over core), row: 8 (over y, z_lo), col: 16 (over x, z_hi).
Axes of the slice: x: 4, y: 4, z: 8 (z_hi: 4, z_lo: 2; z = z_hi * 2 + z_lo), core: 2. Of those that a mesh axis runs over, the one named last changes fastest.
Arguments:
- load: float32 [16, 16, 1024, 256], P(('grp', 'row'), 'col'), may hold values from -6 to 6
- guess: float32 [16, 16, 1024, 256], P(('grp', 'row'), 'col'), may hold values from -6 to 6
- interface_op: bfloat16 [16, 16, 1024, 1024], P(('grp', 'row'), 'col'), may hold values from -1 to 5
- precond: bfloat16 [16, 16, 1024, 1024], P(('grp', 'row'), 'col'), may hold values from -1 to 2
- basis: bfloat16 [16, 16, 1024, 64], P(('grp', 'row'), 'col'), may hold values from -0.375 to 0.375
- coarse_inverse: bfloat16 [16384, 16384], P(('grp', 'row'), 'col'), may hold values from -0.0625 to 0.0625
- edge_rows: int32 [16, 16, 1024], P(('grp', 'row'), 'col'), may hold values from 0 to 1023, each once within a row
- coarse_slot: int32 [16, 16, 64], P(('grp', 'row'), 'col'), may hold values from 0 to 63, each once within a row
Outputs:
- displacement: float32 [16, 16, 1024, 256], P(('grp', 'row'), 'col')
Inputs may be any that keep to these rules, and one draw needn't show every extreme that they name: `edge_rows`: each subdomain lists each of its 1024 interface rows once. `coarse_slot`: each subdomain gives each of its 64 basis vectors a different offset.
All inputs are finite; a program needn't handle non-finite values.
Results may differ from a plain program's by a relative error of at most 0.0095.
Values may be sent and summed in bfloat16 or wider, within the bound.
A program may use at most 64 MiB of HBM per device.

v0:
```python
import jax
import jax.numpy as jnp
from jax import lax
from jax.sharding import PartitionSpec as P

ITERS = 2


OMEGA = 0.6


def extended(shard, sides, width):
    for axis, dim in sides:
        size, length = (lax.axis_size(axis), shard.shape[dim])
        up = [(i, (i + 1) % size) for i in range(size - 1)]
        down = [(j, i) for i, j in up]
        last = lax.slice_in_dim(shard, length - width, length, axis=dim)
        first = lax.slice_in_dim(shard, 0, width, axis=dim)
        before = lax.ppermute(last, axis, up)
        after = lax.ppermute(first, axis, down)
        shard = jnp.concatenate([before, shard, after], axis=dim)
    return shard


def body(load, guess, interface_op, precond, basis, coarse_inverse, edge_rows, coarse_slot):
    local_load = load[0, 0]
    current = guess[0, 0]
    operator_block = interface_op[0, 0]
    precond_block = precond[0, 0]
    basis_block = basis[0, 0]
    row_order = edge_rows[0, 0]
    slot_order = coarse_slot[0, 0]
    n_unknowns, n_cases = local_load.shape
    edge_len = n_unknowns // 4
    n_basis = basis_block.shape[1]
    block_len = coarse_inverse.shape[1]
    grid_rows = lax.axis_size(("grp", "row"))
    grid_cols = lax.axis_size("col")
    my_row = lax.axis_index(("grp", "row"))
    my_col = lax.axis_index("col")
    present = jnp.stack([my_col > 0, my_col < grid_cols - 1, my_row > 0, my_row < grid_rows - 1])
    present = present.astype(jnp.float32)[:, None, None]
    selector = (slot_order[:, None] == jnp.arange(n_basis, dtype=jnp.int32)[None, :]).astype(
        jnp.bfloat16
    )
    contract_first = (((0,), (0,)), ((), ()))

    def place(values):
        blank = jnp.zeros((n_unknowns, n_cases), jnp.float32)
        return blank.at[row_order].set(values.reshape(n_unknowns, n_cases))

    def traces(values):
        own = values[row_order].reshape(4, edge_len, n_cases)
        across_cols = extended(own[0:2], (("col", 0),), 1)
        across_rows = extended(own[2:4], ((("grp", "row"), 0),), 1)
        beside = jnp.stack([across_cols[0], across_cols[3], across_rows[0], across_rows[3]])
        return (own, beside)

    for sweep in range(ITERS):
        applied = jnp.dot(
            operator_block, current.astype(jnp.bfloat16), preferred_element_type=jnp.float32
        )
        own_applied, beside_applied = traces(applied)
        resid = local_load - applied - place(beside_applied)
        resid_bf = resid.astype(jnp.bfloat16)
        local_fix = jnp.dot(precond_block, resid_bf, preferred_element_type=jnp.float32)
        fine_own, fine_beside = traces(local_fix)
        smooth_fix = local_fix + 0.5 * place(present * (fine_beside - fine_own))
        coarse_res = lax.dot_general(
            basis_block, resid_bf, contract_first, preferred_element_type=jnp.float32
        ).astype(jnp.bfloat16)
        ordered = lax.dot_general(
            selector, coarse_res, contract_first, preferred_element_type=jnp.float32
        ).astype(jnp.bfloat16)
        row_block = lax.all_gather(ordered, "col", axis=0, tiled=True)
        source = lax.all_gather(row_block, ("grp", "row"), axis=0, tiled=True)
        offset = my_col * block_len
        column_part = lax.dynamic_slice_in_dim(source, offset, block_len, 0)
        summed = lax.psum_scatter(
            jnp.dot(coarse_inverse, column_part, preferred_element_type=jnp.float32),
            "col",
            scatter_dimension=0,
            tiled=True,
        ).astype(jnp.bfloat16)
        picked = jnp.dot(selector, summed, preferred_element_type=jnp.float32).astype(jnp.bfloat16)
        coarse_fix = jnp.dot(basis_block, picked, preferred_element_type=jnp.float32)
        current = current + OMEGA * (smooth_fix + coarse_fix)
    return current[None, None]


def solution(mesh):
    return jax.shard_map(
        body,
        mesh=mesh,
        in_specs=(
            P(("grp", "row"), "col", None, None),
            P(("grp", "row"), "col", None, None),
            P(("grp", "row"), "col", None, None),
            P(("grp", "row"), "col", None, None),
            P(("grp", "row"), "col", None, None),
            P(("grp", "row"), "col"),
            P(("grp", "row"), "col", None),
            P(("grp", "row"), "col", None),
        ),
        out_specs=P(("grp", "row"), "col", None, None),
        check_vma=False,
    )
```

profile of v0, /device:TPU:1, one launch (start us, length us, event | category | flops | bytes accessed | tf_op | source)
XLA Modules:
  0.0 507.3 jit_solution(4390998081680891761)
XLA Ops:
  10.1 4.7 gather_fusion
  16.0 5.7 %collective-permute-start = (f32[1,256,256]{2,1,0:T(8,128)S(1)}, f32[1,256,256]{2,1,0:T(8,128)S(1)}, u32[]{:S(2)}, u32[]{:S(2)}) collective-permute-start(f32[1,256,256]{2,1,0:T(8,128)S(1)} %get-tuple-element.17), channel_id=1, source_target_pairs={{0,1},{1,2},{2,3},{3,4},{4,5},{5,6},{6,7},{7,8},{8,9},{9,10},{10,1... | collective-permute-start | bytes 786440 | tf_op jit(solution)/shard_map/ppermute | solution.py:19
  21.8 3.5 collective-permute-start.2
  26.6 5.2 %collective-permute-start.3 = (f32[1,256,256]{2,1,0:T(8,128)S(1)}, f32[1,256,256]{2,1,0:T(8,128)S(1)}, u32[]{:S(2)}, u32[]{:S(2)}) collective-permute-start(f32[1,256,256]{2,1,0:T(8,128)S(1)} %get-tuple-element.20), channel_id=1, source_target_pairs={{16,0},{32,16},{48,32},{64,48},{80,64},{96,80},{112,96},{128,112},... | collective-permute-start | bytes 786440 | tf_op jit(solution)/shard_map/ppermute | solution.py:20
  31.9 6.2 %collective-permute-done.2 = f32[1,256,256]{2,1,0:T(8,128)S(1)} collective-permute-done((f32[1,256,256]{2,1,0:T(8,128)S(1)}, f32[1,256,256]{2,1,0:T(8,128)S(1)}, u32[]{:S(2)}, u32[]{:S(2)}) %collective-permute-start.2) | collective-permute-done | bytes 262176 | tf_op jit(solution)/shard_map/ppermute | solution.py:19
  38.0 4.7 collective-permute-done.3
  43.8 6.3 %scatter_custom_fusion = f32[1024,256]{1,0:T(8,128)} fusion(s32[1024]{0:T(1024)S(1)} %bitcast.145, f32[1024,256]{1,0:T(8,128)} %bitcast.140, f32[]{:T(128)} %constant.12.clone.1), kind=kCustom, calls=%fused_computation.60 | custom fusion | bytes 1049088 | tf_op jit(solution)/shard_map/scatter | solution.py:50
  54.0 47.8 %all_gather.12 = bf16[1024,256]{1,0:T(8,128)(2,1)} all-gather(bf16[64,256]{1,0:T(8,128)(2,1)S(1)} %convolution_convert_fusion.5), channel_id=1, replica_groups=mesh['grp'=2,'row'=8,'col'=16] {'col'}, dimensions={0}, use_global_device_ids=true | all-gather | bytes 557056 | tf_op jit(solution)/shard_map/all_gather | solution.py:75
  101.9 56.4 %all-gather.3.cloned.1.call-done = bf16[16384,256]{1,0:T(8,128)(2,1)} async-done(((bf16[1024,256]{1,0:T(8,128)(2,1)}), bf16[16384,256]{1,0:T(8,128)(2,1)}) %all-gather.3.cloned.1.call-update) | async-done | bytes 8388624 | tf_op jit(solution)/shard_map/all_gather | solution.py:76
  164.6 4.7 gather_fusion.1
  170.6 4.2 collective-permute-start.4
  174.8 5.0 collective-permute-start.7
  183.2 11.1 %collective-permute-done.7 = f32[1,256,256]{2,1,0:T(8,128)S(1)} collective-permute-done((f32[1,256,256]{2,1,0:T(8,128)S(1)}, f32[1,256,256]{2,1,0:T(8,128)S(1)}, u32[]{:S(2)}, u32[]{:S(2)}) %collective-permute-start.7) | collective-permute-done | bytes 262176 | tf_op jit(solution)/shard_map/ppermute | solution.py:20
  194.3 3.8 collective-permute-done.6
  199.4 6.3 %scatter_custom_fusion.1 = f32[1024,256]{1,0:T(8,128)} fusion(s32[1024]{0:T(1024)S(1)} %bitcast.146, f32[1024,256]{1,0:T(8,128)} %fusion.25, f32[]{:T(128)} %constant.12.clone.1), kind=kCustom, calls=%fused_computation.58 | custom fusion | bytes 1049088 | tf_op jit(solution)/shard_map/scatter | solution.py:50
  205.7 47.5 %reduce-scatter.7.cloned.1.call-done = f32[64,256]{1,0:T(8,128)} async-done(((f32[1024,256]{1,0:T(8,128)}), f32[64,256]{1,0:T(8,128)}) %reduce-scatter.7.cloned.1.call-update) | async-done | bytes 65552
  254.1 3.0 fusion.21
  259.1 4.7 gather_fusion.2
  265.0 3.1 collective-permute-start.8
  271.7 7.1 %collective-permute-start.11 = (f32[1,256,256]{2,1,0:T(8,128)S(1)}, f32[1,256,256]{2,1,0:T(8,128)S(1)}, u32[]{:S(2)}, u32[]{:S(2)}) collective-permute-start(f32[1,256,256]{2,1,0:T(8,128)S(1)} %get-tuple-element.12), channel_id=1, source_target_pairs={{16,0},{32,16},{48,32},{64,48},{80,64},{96,80},{112,96},{128,112},... | collective-permute-start | bytes 786440 | tf_op jit(solution)/shard_map/ppermute | solution.py:20
  278.8 7.4 %collective-permute-done.10 = f32[1,256,256]{2,1,0:T(8,128)S(1)} collective-permute-done((f32[1,256,256]{2,1,0:T(8,128)S(1)}, f32[1,256,256]{2,1,0:T(8,128)S(1)}, u32[]{:S(2)}, u32[]{:S(2)}) %collective-permute-start.10) | collective-permute-done | bytes 262176 | tf_op jit(solution)/shard_map/ppermute | solution.py:19
  289.4 6.3 %scatter_custom_fusion.2 = f32[1024,256]{1,0:T(8,128)} fusion(s32[1024]{0:T(1024)S(1)} %bitcast.147, f32[1024,256]{1,0:T(8,128)} %bitcast.141, f32[]{:T(128)} %constant.12.clone.1), kind=kCustom, calls=%fused_computation.56 | custom fusion | bytes 1049088 | tf_op jit(solution)/shard_map/scatter | solution.py:50
  299.6 44.8 %all_gather.14 = bf16[1024,256]{1,0:T(8,128)(2,1)} all-gather(bf16[64,256]{1,0:T(8,128)(2,1)S(1)} %convolution_convert_fusion.3), channel_id=1, replica_groups=mesh['grp'=2,'row'=8,'col'=16] {'col'}, dimensions={0}, use_global_device_ids=true | all-gather | bytes 557056 | tf_op jit(solution)/shard_map/all_gather | solution.py:75
  344.5 57.6 %all-gather.5.cloned.1.call-done = bf16[16384,256]{1,0:T(8,128)(2,1)} async-done(((bf16[1024,256]{1,0:T(8,128)(2,1)}), bf16[16384,256]{1,0:T(8,128)(2,1)}) %all-gather.5.cloned.1.call-update) | async-done | bytes 8388624 | tf_op jit(solution)/shard_map/all_gather | solution.py:76
  408.4 4.7 gather_fusion.3
  414.4 4.2 collective-permute-start.12
  418.6 5.0 collective-permute-start.15
  426.8 11.3 %collective-permute-done.15 = f32[1,256,256]{2,1,0:T(8,128)S(1)} collective-permute-done((f32[1,256,256]{2,1,0:T(8,128)S(1)}, f32[1,256,256]{2,1,0:T(8,128)S(1)}, u32[]{:S(2)}, u32[]{:S(2)}) %collective-permute-start.15) | collective-permute-done | bytes 262176 | tf_op jit(solution)/shard_map/ppermute | solution.py:20
  438.2 3.7 collective-permute-done.14
  443.1 6.3 %scatter_custom_fusion.3 = f32[1024,256]{1,0:T(8,128)} fusion(s32[1024]{0:T(1024)S(1)} %bitcast.148, f32[1024,256]{1,0:T(8,128)} %fusion.24, f32[]{:T(128)} %constant.12.clone.1), kind=kCustom, calls=%fused_computation.54 | custom fusion | bytes 1049088 | tf_op jit(solution)/shard_map/scatter | solution.py:50
  449.4 47.4 %reduce-scatter.9.cloned.1.call-done = f32[64,256]{1,0:T(8,128)} async-done(((f32[1024,256]{1,0:T(8,128)}), f32[64,256]{1,0:T(8,128)}) %reduce-scatter.9.cloned.1.call-update) | async-done | bytes 65552
  497.7 3.0 fusion.23
  (63 shorter events, 51.3 us)
Async XLA Ops:
  6.5 1.6 copy-start
  6.5 151.7 %all-gather.3.cloned.1.call-start = ((), (), s32[]{:S(2)}) async-start(), calls=%async_computation.2 | async-start | bytes 8912896 | tf_op jit(solution)/shard_map/all_gather | solution.py:76
  16.0 15.8 %collective-permute-start = (f32[1,256,256]{2,1,0:T(8,128)S(1)}, f32[1,256,256]{2,1,0:T(8,128)S(1)}, u32[]{:S(2)}, u32[]{:S(2)}) collective-permute-start(f32[1,256,256]{2,1,0:T(8,128)S(1)} %get-tuple-element.17), channel_id=1, source_target_pairs={{0,1},{1,2},{2,3},{3,4},{4,5},{5,6},{6,7},{7,8},{8,9},{9,10},{10,1... | collective-permute-start | bytes 786440 | tf_op jit(solution)/shard_map/ppermute | solution.py:19
  21.8 16.3 %collective-permute-start.2 = (f32[1,256,256]{2,1,0:T(8,128)S(1)}, f32[1,256,256]{2,1,0:T(8,128)S(1)}, u32[]{:S(2)}, u32[]{:S(2)}) collective-permute-start(f32[1,256,256]{2,1,0:T(8,128)S(1)} %get-tuple-element.18), channel_id=1, source_target_pairs={{0,16},{16,32},{32,48},{48,64},{64,80},{80,96},{96,112},{112,128},... | collective-permute-start | bytes 786440 | tf_op jit(solution)/shard_map/ppermute | solution.py:19
  25.3 12.7 %collective-permute-start.1 = (f32[1,256,256]{2,1,0:T(8,128)S(1)}, f32[1,256,256]{2,1,0:T(8,128)S(1)}, u32[]{:S(2)}, u32[]{:S(2)}) collective-permute-start(f32[1,256,256]{2,1,0:T(8,128)S(1)} %get-tuple-element.19), channel_id=1, source_target_pairs={{1,0},{2,1},{3,2},{4,3},{5,4},{6,5},{7,6},{8,7},{9,8},{10,9},{11,1... | collective-permute-start | bytes 786440 | tf_op jit(solution)/shard_map/ppermute | solution.py:20
  26.6 16.1 %collective-permute-start.3 = (f32[1,256,256]{2,1,0:T(8,128)S(1)}, f32[1,256,256]{2,1,0:T(8,128)S(1)}, u32[]{:S(2)}, u32[]{:S(2)}) collective-permute-start(f32[1,256,256]{2,1,0:T(8,128)S(1)} %get-tuple-element.20), channel_id=1, source_target_pairs={{16,0},{32,16},{48,32},{64,48},{80,64},{96,80},{112,96},{128,112},... | collective-permute-start | bytes 786440 | tf_op jit(solution)/shard_map/ppermute | solution.py:20
  50.1 2.5 copy-start.3
  50.1 2.5 copy-start.4
  101.8 151.3 %reduce-scatter.7.cloned.1.call-start = ((), (), s32[]{:S(2)}) async-start(), calls=%async_computation.4 | async-start | bytes 1114112
  162.1 239.9 %all-gather.5.cloned.1.call-start = ((), (), s32[]{:S(2)}) async-start(), calls=%async_computation.3 | async-start | bytes 8912896 | tf_op jit(solution)/shard_map/all_gather | solution.py:76
  169.3 28.9 %copy-start.1 = (f32[1024,256]{1,0:T(8,128)S(1)}, f32[1024,256]{1,0:T(8,128)}, u32[]{:S(2)}) copy-start(f32[1024,256]{1,0:T(8,128)} %gather_fusion.1) | copy-start | bytes 3145732
  170.6 12.6 %collective-permute-start.4 = (f32[1,256,256]{2,1,0:T(8,128)S(1)}, f32[1,256,256]{2,1,0:T(8,128)S(1)}, u32[]{:S(2)}, u32[]{:S(2)}) collective-permute-start(f32[1,256,256]{2,1,0:T(8,128)S(1)} %get-tuple-element.13), channel_id=1, source_target_pairs={{0,1},{1,2},{2,3},{3,4},{4,5},{5,6},{6,7},{7,8},{8,9},{9,10},{10,1... | collective-permute-start | bytes 786440 | tf_op jit(solution)/shard_map/ppermute | solution.py:19
  174.8 19.5 %collective-permute-start.7 = (f32[1,256,256]{2,1,0:T(8,128)S(1)}, f32[1,256,256]{2,1,0:T(8,128)S(1)}, u32[]{:S(2)}, u32[]{:S(2)}) collective-permute-start(f32[1,256,256]{2,1,0:T(8,128)S(1)} %get-tuple-element.14), channel_id=1, source_target_pairs={{16,0},{32,16},{48,32},{64,48},{80,64},{96,80},{112,96},{128,112},... | collective-permute-start | bytes 786440 | tf_op jit(solution)/shard_map/ppermute | solution.py:20
  179.8 18.3 %collective-permute-start.6 = (f32[1,256,256]{2,1,0:T(8,128)S(1)}, f32[1,256,256]{2,1,0:T(8,128)S(1)}, u32[]{:S(2)}, u32[]{:S(2)}) collective-permute-start(f32[1,256,256]{2,1,0:T(8,128)S(1)} %get-tuple-element.15), channel_id=1, source_target_pairs={{0,16},{16,32},{32,48},{48,64},{64,80},{80,96},{96,112},{112,128},... | collective-permute-start | bytes 786440 | tf_op jit(solution)/shard_map/ppermute | solution.py:19
  181.8 16.4 %collective-permute-start.5 = (f32[1,256,256]{2,1,0:T(8,128)S(1)}, f32[1,256,256]{2,1,0:T(8,128)S(1)}, u32[]{:S(2)}, u32[]{:S(2)}) collective-permute-start(f32[1,256,256]{2,1,0:T(8,128)S(1)} %get-tuple-element.16), channel_id=1, source_target_pairs={{1,0},{2,1},{3,2},{4,3},{5,4},{6,5},{7,6},{8,7},{9,8},{10,9},{11,1... | collective-permute-start | bytes 786440 | tf_op jit(solution)/shard_map/ppermute | solution.py:20
  265.0 13.8 %collective-permute-start.8 = (f32[1,256,256]{2,1,0:T(8,128)S(1)}, f32[1,256,256]{2,1,0:T(8,128)S(1)}, u32[]{:S(2)}, u32[]{:S(2)}) collective-permute-start(f32[1,256,256]{2,1,0:T(8,128)S(1)} %get-tuple-element.9), channel_id=1, source_target_pairs={{0,1},{1,2},{2,3},{3,4},{4,5},{5,6},{6,7},{7,8},{8,9},{9,10},{10,1... | collective-permute-start | bytes 786440 | tf_op jit(solution)/shard_map/ppermute | solution.py:19
  268.1 18.1 %collective-permute-start.10 = (f32[1,256,256]{2,1,0:T(8,128)S(1)}, f32[1,256,256]{2,1,0:T(8,128)S(1)}, u32[]{:S(2)}, u32[]{:S(2)}) collective-permute-start(f32[1,256,256]{2,1,0:T(8,128)S(1)} %get-tuple-element.10), channel_id=1, source_target_pairs={{0,16},{16,32},{32,48},{48,64},{64,80},{80,96},{96,112},{112,128},... | collective-permute-start | bytes 786440 | tf_op jit(solution)/shard_map/ppermute | solution.py:19
  270.4 15.8 %collective-permute-start.9 = (f32[1,256,256]{2,1,0:T(8,128)S(1)}, f32[1,256,256]{2,1,0:T(8,128)S(1)}, u32[]{:S(2)}, u32[]{:S(2)}) collective-permute-start(f32[1,256,256]{2,1,0:T(8,128)S(1)} %get-tuple-element.11), channel_id=1, source_target_pairs={{1,0},{2,1},{3,2},{4,3},{5,4},{6,5},{7,6},{8,7},{9,8},{10,9},{11,1... | collective-permute-start | bytes 786440 | tf_op jit(solution)/shard_map/ppermute | solution.py:20
  271.7 16.6 %collective-permute-start.11 = (f32[1,256,256]{2,1,0:T(8,128)S(1)}, f32[1,256,256]{2,1,0:T(8,128)S(1)}, u32[]{:S(2)}, u32[]{:S(2)}) collective-permute-start(f32[1,256,256]{2,1,0:T(8,128)S(1)} %get-tuple-element.12), channel_id=1, source_target_pairs={{16,0},{32,16},{48,32},{64,48},{80,64},{96,80},{112,96},{128,112},... | collective-permute-start | bytes 786440 | tf_op jit(solution)/shard_map/ppermute | solution.py:20
  344.5 152.3 %reduce-scatter.9.cloned.1.call-start = ((), (), s32[]{:S(2)}) async-start(), calls=%async_computation.5 | async-start | bytes 1114112
  413.0 28.9 %copy-start.2 = (f32[1024,256]{1,0:T(8,128)S(1)}, f32[1024,256]{1,0:T(8,128)}, u32[]{:S(2)}) copy-start(f32[1024,256]{1,0:T(8,128)} %gather_fusion.3) | copy-start | bytes 3145732
  414.4 12.4 %collective-permute-start.12 = (f32[1,256,256]{2,1,0:T(8,128)S(1)}, f32[1,256,256]{2,1,0:T(8,128)S(1)}, u32[]{:S(2)}, u32[]{:S(2)}) collective-permute-start(f32[1,256,256]{2,1,0:T(8,128)S(1)} %get-tuple-element.5), channel_id=1, source_target_pairs={{0,1},{1,2},{2,3},{3,4},{4,5},{5,6},{6,7},{7,8},{8,9},{9,10},{10,1... | collective-permute-start | bytes 786440 | tf_op jit(solution)/shard_map/ppermute | solution.py:19
  418.6 19.6 %collective-permute-start.15 = (f32[1,256,256]{2,1,0:T(8,128)S(1)}, f32[1,256,256]{2,1,0:T(8,128)S(1)}, u32[]{:S(2)}, u32[]{:S(2)}) collective-permute-start(f32[1,256,256]{2,1,0:T(8,128)S(1)} %get-tuple-element.6), channel_id=1, source_target_pairs={{16,0},{32,16},{48,32},{64,48},{80,64},{96,80},{112,96},{128,112},... | collective-permute-start | bytes 786440 | tf_op jit(solution)/shard_map/ppermute | solution.py:20
  423.6 18.3 %collective-permute-start.14 = (f32[1,256,256]{2,1,0:T(8,128)S(1)}, f32[1,256,256]{2,1,0:T(8,128)S(1)}, u32[]{:S(2)}, u32[]{:S(2)}) collective-permute-start(f32[1,256,256]{2,1,0:T(8,128)S(1)} %get-tuple-element.7), channel_id=1, source_target_pairs={{0,16},{16,32},{32,48},{48,64},{64,80},{80,96},{96,112},{112,128},... | collective-permute-start | bytes 786440 | tf_op jit(solution)/shard_map/ppermute | solution.py:19
  425.5 16.3 %collective-permute-start.13 = (f32[1,256,256]{2,1,0:T(8,128)S(1)}, f32[1,256,256]{2,1,0:T(8,128)S(1)}, u32[]{:S(2)}, u32[]{:S(2)}) collective-permute-start(f32[1,256,256]{2,1,0:T(8,128)S(1)} %get-tuple-element.8), channel_id=1, source_target_pairs={{1,0},{2,1},{3,2},{4,3},{5,4},{6,5},{7,6},{8,7},{9,8},{10,9},{11,1... | collective-permute-start | bytes 786440 | tf_op jit(solution)/shard_map/ppermute | solution.py:20
Sparse Core Ops, SparseCore 0:
  101.9 56.2 all-gather.2
  162.3 90.8 reduce-scatter.6
  344.6 57.4 all-gather.4
  406.1 90.6 reduce-scatter.8
where the time goes:
time: 510 us; the launch traced here: 507 us
  waiting for transfers between devices  259 us (51%)
  blocking collectives  92.6 us (18%)
  starting transfers between devices  54.5 us (11%)
  local copies, waits for them, and re-layouts  54.4 us (11%)
  matrix products  22.4 us (4%)
  between operations  13.4 us (3%)
  other arithmetic  10.6 us (2%)
    all_gather x2, waiting for transfers between devices, body(): source = lax.all_gather(row_block, ('grp', 'row'), axis=0, tiled=True)  114 us
    unnamed x6, waiting for transfers between devices  94.9 us
    all_gather x2, blocking collectives, body(): row_block = lax.all_gather(ordered, 'col', axis=0, tiled=True)  92.6 us
    ppermute x8, waiting for transfers between devices, extended(): after = lax.ppermute(first, axis, down)  29.3 us
    ppermute x8, starting transfers between devices, extended(): after = lax.ppermute(first, axis, down)  27.4 us
    ppermute x8, starting transfers between devices, extended(): before = lax.ppermute(last, axis, up)  26.9 us
    scatter x4, local copies, waits for them, and re-layouts, place(): return blank.at[row_order].set(values.reshape(n_unknowns, n_cases))  25.1 us
    ppermute x8, waiting for transfers between devices, extended(): before = lax.ppermute(last, axis, up)  21.1 us
  transfers between devices with their start and end apart: 20, of which 12 were waited for; matrix products, arithmetic and copies ran while one was open for 6% of the time, Pallas kernels for 0%

commit v1 on v0

v1 whole, which is shorter than its diff:
```python
import jax
import jax.numpy as jnp
from jax import lax
from jax.experimental import pallas as pl
from jax.experimental.pallas import tpu as pltpu
from jax.sharding import PartitionSpec as P

ITERS = 2
OMEGA = 0.6
MESH = pl.DeviceIdType.MESH
BF = jnp.bfloat16
F32 = jnp.float32
TILE = 256


def mm(left, right):
    return jnp.dot(left, right, preferred_element_type=F32)


def mm_nt(left, right):
    return lax.dot_general(left, right, (((1,), (1,)), ((), ())), preferred_element_type=F32)


def kernel(
    load_h, guess_h, op_h, pre_h, basis_h, coarse_h, rows_h, slot_h, out_h,
    u, load, amat, mmat, cmat, basis, rows, slot,
    pick, place, b2, b2t, keep, ub, applied, resid, fix,
    esend, erecv, cres, gath, ypart, yown, xrecv, zpart, zown, zrecv,
    in_sem, out_sem, e_ss, e_rs, t_ss, t_rs, y_ss, y_rs, p_ss, p_rs, x_ss, x_rs, z_ss, z_rs,
):
    core = lax.axis_index("grp")
    row = lax.axis_index("row")
    col = lax.axis_index("col")
    y, zl = row // 2, lax.rem(row, 2)
    x, zh = col // 4, lax.rem(col, 4)
    a = core * 8 + row
    n_basis = basis.shape[1]

    def at_row(r, c):
        return {"grp": r // 8, "row": lax.rem(r, 8), "col": c}

    loads = [
        pltpu.make_async_copy(src, dst, in_sem.at[i])
        for i, (src, dst) in enumerate(
            [
                (rows_h.at[0], rows),
                (guess_h.at[0, 0], u),
                (op_h.at[0, 0], amat),
                (load_h.at[0, 0], load),
                (slot_h.at[0], slot),
                (basis_h.at[0, 0], basis),
                (pre_h.at[0, 0], mmat),
                (coarse_h, cmat),
            ]
        )
    ]
    for c in loads:
        c.start()
    l_rows, l_u, l_a, l_load, l_slot, l_basis, l_m, l_c = loads

    present = [col > 0, col < 15, a > 0, a < 15]
    across = [at_row(a, col - 1), at_row(a, col + 1), at_row(a - 1, col), at_row(a + 1, col)]
    off_diag = a != col
    mirror = at_row(col, a)
    y_peer = [{"grp": core, "row": lax.rem(y + d, 4) * 2 + zl, "col": col} for d in (1, 2, 3)]
    z_pair = {"grp": core, "row": y * 2 + 1 - zl, "col": col}
    c_pair = {"grp": 1 - core, "row": row, "col": col}
    x_peer = [{"grp": core, "row": row, "col": lax.rem(x + d, 4) * 4 + zh} for d in (1, 2, 3)]
    h_peer = [{"grp": core, "row": row, "col": x * 4 + lax.rem(zh + d, 4)} for d in (1, 2, 3)]

    barrier = pltpu.get_barrier_semaphore()
    fixed = y_peer + [z_pair, c_pair] + x_peer + h_peer
    for peer in fixed:
        pl.semaphore_signal(barrier, inc=1, device_id=peer, device_id_type=MESH)
    for ok, peer in zip(present + [off_diag], across + [mirror]):
        @pl.when(ok)
        def _():
            pl.semaphore_signal(barrier, inc=1, device_id=peer, device_id_type=MESH)

    for k in range(4):
        @pl.when(jnp.logical_not(present[k]))
        def _():
            for e in range(2 * ITERS):
                erecv[e, k] = jnp.zeros(erecv.shape[2:], BF)

    l_rows.wait()
    ni = pick.shape[0]

    @pl.loop(0, ni // 128)
    def _(t):
        base = pl.multiple_of(t * 128, 128)
        here = rows[:, pl.ds(base, 128)].astype(F32)
        down = jnp.broadcast_to(here, (128, 128)).T.astype(jnp.int32)
        lane = lax.broadcasted_iota(jnp.int32, (128, 128), 1)
        for v in range(ni // 128):
            pick[pl.ds(base, 128), v * 128:(v + 1) * 128] = jnp.where(
                down == lane + v * 128, 1.0, 0.0
            ).astype(BF)
        sub = lax.broadcasted_iota(jnp.int32, (128, ni), 0) + base
        place[pl.ds(base, 128), :] = jnp.where(sub == rows[...], 1.0, 0.0).astype(BF)

    def tiles(body):
        @pl.loop(0, ni // TILE)
        def _(t):
            body(pl.ds(pl.multiple_of(t * TILE, TILE), TILE))

    flag = jnp.concatenate(
        [jnp.full((TILE, 128), p.astype(F32)) for p in present], axis=0
    ).astype(BF)

    def keep_tile(at):
        keep[at, :] = 1.0 - 0.5 * mm(place[at, :], flag)

    tiles(keep_tile)

    l_u.wait()
    ub[...] = u[...].astype(BF)

    l_slot.wait()
    l_basis.wait()
    order = (lax.broadcasted_iota(jnp.int32, (n_basis, n_basis), 0) == slot[...])
    order = jnp.where(order, 1.0, 0.0).astype(BF)
    b2t[...] = mm_nt(order, basis[...]).astype(BF)
    b2[...] = mm_nt(basis[...], order).astype(BF)

    l_a.wait()

    total = 11 + sum(p.astype(jnp.int32) for p in present) + off_diag.astype(jnp.int32)
    pl.semaphore_wait(barrier, total)

    def edge_copy(e, k):
        return pltpu.make_async_remote_copy(
            src_ref=esend.at[e, k], dst_ref=erecv.at[e, k ^ 1],
            send_sem=e_ss.at[e, k], recv_sem=e_rs.at[e, k ^ 1],
            device_id=across[k], device_id_type=MESH,
        )

    def edge_arrival(e, k):
        return pltpu.make_async_remote_copy(
            src_ref=esend.at[e, k], dst_ref=erecv.at[e, k],
            send_sem=e_ss.at[e, k], recv_sem=e_rs.at[e, k],
            device_id=across[k], device_id_type=MESH,
        )

    def send_edges(e, source):
        for k in (0, 1, 2, 3):
            esend[e, k] = mm(pick[k * TILE:(k + 1) * TILE, :], source).astype(BF)

            @pl.when(present[k])
            def _():
                edge_copy(e, k).start()

    def take_edges(e):
        for k in range(4):
            @pl.when(present[k])
            def _():
                edge_arrival(e, k).wait_recv()

    def beside(e):
        return erecv[e].reshape(ni, erecv.shape[3])

    for s in range(ITERS):
        e1, e2 = 2 * s, 2 * s + 1

        def apply_tile(at):
            value = mm(amat[at, :], ub[...])
            applied[at, :] = value
            resid[at, :] = value.astype(BF)

        tiles(apply_tile)
        send_edges(e1, resid[...])
        if s == 0:
            l_load.wait()
        take_edges(e1)

        def resid_tile(at):
            value = load[at, :] - applied[at, :] - mm(place[at, :], beside(e1))
            resid[at, :] = value.astype(BF)

        tiles(resid_tile)

        cres[s] = mm(b2t[...], resid[...]).astype(BF)
        crossing = pltpu.make_async_remote_copy(
            src_ref=cres.at[s],
            dst_ref=gath.at[s, col // 8, lax.rem(col, 8) // 2, lax.rem(col, 2)],
            send_sem=t_ss.at[s], recv_sem=t_rs.at[s],
            device_id=mirror, device_id_type=MESH,
        )

        @pl.when(off_diag)
        def _():
            crossing.start()

        @pl.when(jnp.logical_not(off_diag))
        def _():
            gath[s, core, y, zl] = cres[s]

        if s == 0:
            l_m.wait()

        def fix_tile(at):
            value = mm(mmat[at, :], resid[...])
            fix[at, :] = value
            applied[at, :] = value

        tiles(fix_tile)

        @pl.when(off_diag)
        def _():
            crossing.wait_recv()

        mine = gath.at[s, core, y, zl]
        y_copies = [
            pltpu.make_async_remote_copy(
                src_ref=mine, dst_ref=mine,
                send_sem=y_ss.at[s, d], recv_sem=y_rs.at[s, d],
                device_id=y_peer[d], device_id_type=MESH,
            )
            for d in range(3)
        ]
        for c in y_copies:
            c.start()
        for c in y_copies:
            c.wait_recv()
        group = gath.at[s, core, :, zl]
        others = gath.at[s, core, :, 1 - zl]

        def pair_copy(i, ref, peer):
            return pltpu.make_async_remote_copy(
                src_ref=ref, dst_ref=ref,
                send_sem=p_ss.at[s, i], recv_sem=p_rs.at[s, i],
                device_id=peer, device_id_type=MESH,
            )

        z_copy = pair_copy(0, group, z_pair)
        c_copy = pair_copy(1, group, c_pair)
        o_copy = pair_copy(2, others, c_pair)
        z_copy.start()
        c_copy.start()

        ub[...] = fix[...].astype(BF)
        send_edges(e2, ub[...])

        z_copy.wait_recv()
        o_copy.start()
        c_copy.wait_recv()
        o_copy.wait_recv()
        if s == 0:
            l_c.wait()
        vec = gath[s].reshape(ni, gath.shape[5])

        x_copies = []
        for d in (2, 1, 3, 0):
            to = lax.rem(x + d, 4)
            block = mm(cmat[pl.ds(pl.multiple_of(to * TILE, TILE), TILE), :], vec)
            if d == 0:
                yown[...] = block
            else:
                ypart[s, d - 1] = block.astype(BF)
                c = pltpu.make_async_remote_copy(
                    src_ref=ypart.at[s, d - 1], dst_ref=xrecv.at[s, d - 1],
                    send_sem=x_ss.at[s, d - 1], recv_sem=x_rs.at[s, d - 1],
                    device_id=x_peer[d - 1], device_id_type=MESH,
                )
                c.start()
                x_copies.append(c)
        for c in x_copies:
            c.wait_recv()
        total_x = yown[...]
        for d in range(3):
            total_x = total_x + xrecv[s, d].astype(F32)
        total_x = total_x.reshape(zown.shape)
        zown[...] = total_x
        zpart[s] = total_x.astype(BF)
        h_copies = [
            pltpu.make_async_remote_copy(
                src_ref=zpart.at[s, lax.rem(zh + d + 1, 4)], dst_ref=zrecv.at[s, d],
                send_sem=z_ss.at[s, d], recv_sem=z_rs.at[s, d],
                device_id=h_peer[d], device_id_type=MESH,
            )
            for d in range(3)
        ]
        for c in h_copies:
            c.start()
        take_edges(e2)

        def smooth_tile(at):
            weight = jnp.concatenate([keep[at, :]] * 2, axis=1)
            fix[at, :] = weight * fix[at, :] + 0.5 * mm(place[at, :], beside(e2))

        tiles(smooth_tile)
        for c in h_copies:
            c.wait_recv()
        sol = zown[zh]
        for d in range(3):
            sol = sol + zrecv[s, d].astype(F32)
        sol = sol.astype(BF)

        def update_tile(at):
            value = u[at, :] + OMEGA * (fix[at, :] + mm(b2[at, :], sol))
            u[at, :] = value
            ub[at, :] = value.astype(BF)

        tiles(update_tile)

        @pl.when(off_diag)
        def _():
            crossing.wait_send()
        for c in y_copies + [z_copy, c_copy, o_copy] + x_copies + h_copies:
            c.wait_send()
        for e in (e1, e2):
            for k in range(4):
                @pl.when(present[k])
                def _():
                    edge_copy(e, k).wait_send()

    done = pltpu.make_async_copy(u, out_h.at[0, 0], out_sem)
    done.start()
    done.wait()


def body(load, guess, interface_op, precond, basis, coarse_inverse, edge_rows, coarse_slot):
    ni, cases = load.shape[2:]
    nb = basis.shape[3]
    dma = pltpu.SemaphoreType.DMA
    vm = pltpu.VMEM
    anywhere = pl.BlockSpec(memory_space=pl.ANY)
    return pl.pallas_call(
        kernel,
        out_shape=jax.ShapeDtypeStruct(load.shape, F32),
        in_specs=[anywhere] * 8,
        out_specs=anywhere,
        scratch_shapes=[
            vm((ni, cases), F32), vm((ni, cases), F32),
            vm((ni, ni), BF), vm((ni, ni), BF), vm((ni, ni), BF),
            vm((ni, nb), BF), vm((1, ni), jnp.int32), vm((1, nb), jnp.int32),
            vm((ni, ni), BF), vm((ni, ni), BF), vm((ni, nb), BF), vm((nb, ni), BF),
            vm((ni, 128), F32), vm((ni, cases), BF), vm((ni, cases), F32),
            vm((ni, cases), BF), vm((ni, cases), F32),
            vm((2 * ITERS, 4, ni // 4, cases), BF), vm((2 * ITERS, 4, ni // 4, cases), BF),
            vm((ITERS, nb, cases), BF), vm((ITERS, 2, 4, 2, nb, cases), BF),
            vm((ITERS, 3, TILE, cases), BF), vm((TILE, cases), F32),
            vm((ITERS, 3, TILE, cases), BF),
            vm((ITERS, 4, nb, cases), BF), vm((4, nb, cases), F32), vm((ITERS, 3, nb, cases), BF),
            dma((8,)), dma,
            dma((2 * ITERS, 4)), dma((2 * ITERS, 4)),
            dma((ITERS,)), dma((ITERS,)),
            dma((ITERS, 3)), dma((ITERS, 3)),
            dma((ITERS, 3)), dma((ITERS, 3)),
            dma((ITERS, 3)), dma((ITERS, 3)),
            dma((ITERS, 3)), dma((ITERS, 3)),
        ],
        compiler_params=pltpu.CompilerParams(
            collective_id=0, has_side_effects=True, vmem_limit_bytes=48 * 1024 * 1024
        ),
    )(load, guess, interface_op, precond, basis, coarse_inverse, edge_rows, coarse_slot)


def solution(mesh):
    cells = (("grp", "row"), "col")
    return jax.shard_map(
        body,
        mesh=mesh,
        in_specs=(
            P(*cells, None, None),
            P(*cells, None, None),
            P(*cells, None, None),
            P(*cells, None, None),
            P(*cells, None, None),
            P(*cells),
            P(*cells, None),
            P(*cells, None),
        ),
        out_specs=P(*cells, None, None),
        check_vma=False,
    )
```

time: 510 us -> 115 us (0.23)
  waiting for transfers between devices: 259 us -> 0 us
  Pallas kernels: 0 us -> 107 us
  blocking collectives: 92.6 us -> 0 us
  starting transfers between devices: 54.5 us -> 0 us
  local copies, waits for them, and re-layouts: 54.4 us -> 7.42 us
  matrix products: 22.4 us -> 0 us
  between operations: 13.4 us -> 0.03 us
  other arithmetic: 10.6 us -> 0 us
    all_gather x2 -> x0, waiting for transfers between devices: 114 us -> none  [body(): source = lax.all_gather(row_block, ('grp', 'row'), axis=0, tiled=True)]
    pallas_call x0 -> x1, Pallas kernels: none -> 107 us  [body(): pl.pallas_call(kernel, out_shape=jax.ShapeDtypeStruct(load.shape, F32), i...]
    unnamed x6 -> x0, waiting for transfers between devices: 94.9 us -> none
    all_gather x2 -> x0, blocking collectives: 92.6 us -> none  [body(): row_block = lax.all_gather(ordered, 'col', axis=0, tiled=True)]
    ppermute x16 -> x0, starting transfers between devices: 54.3 us -> none  [the longest x8 27.4 us: extended(): after = lax.ppermute(first, axis, down)]
    ppermute x16 -> x0, waiting for transfers between devices: 50.4 us -> none  [the longest x8 29.3 us: extended(): after = lax.ppermute(first, axis, down)]
    scatter x4 -> x0, local copies, waits for them, and re-layouts: 25.1 us -> none  [place(): return blank.at[row_order].set(values.reshape(n_unknowns, n_cases))]
    dot_general x10 -> x0, matrix products: 22.4 us -> none  [the longest x2 6.04 us: body(): jnp.dot(basis_block, picked, preferred_element_type=jnp.float32)]
  transfers between devices with their start and end apart: 20 -> 0, of which waited for: 12 -> 0; matrix products, arithmetic and copies ran while one was open for 6% -> 0% of each run, Pallas kernels for 0% -> 0%
where the time goes in v1:
time: 115 us; the launch traced here: 114 us
  Pallas kernels  107 us (93%)
  local copies, waits for them, and re-layouts  7.42 us (6%)
    pallas_call x1, Pallas kernels, body(): pl.pallas_call(kernel, out_shape=jax.ShapeDtypeStruct(load.shape, F32), i...  107 us
    unnamed x12, local copies, waits for them, and re-layouts  7.42 us

profile of v1, /device:TPU:1, one launch (start us, length us, event | category | flops | bytes accessed | tf_op | source)
XLA Modules:
  0.0 114.1 jit_solution(9463029778095510782)
XLA Ops:
  0.0 1.1 copy.9.basis_h
  1.1 0.0 copy-start
  1.1 1.6 %copy-done = bf16[1,1,1024,1024]{3,2,1,0:T(8,128)(2,1)S(1)} copy-done((bf16[1,1,1024,1024]{3,2,1,0:T(8,128)(2,1)S(1)}, bf16[1,1,1024,1024]{3,2,1,0:T(8,128)(2,1)}, u32[]{:S(2)}) %copy-start) | copy-done | bytes 2097176
  2.7 0.0 copy-start.1
  2.7 1.2 %copy-done.1 = f32[1,1,1024,256]{3,2,1,0:T(8,128)S(1)} copy-done((f32[1,1,1024,256]{3,2,1,0:T(8,128)S(1)}, f32[1,1,1024,256]{3,2,1,0:T(8,128)}, u32[]{:S(2)}) %copy-start.1) | copy-done | bytes 1048600
  3.9 0.0 copy-start.2
  3.9 1.2 %copy-done.2 = f32[1,1,1024,256]{3,2,1,0:T(8,128)S(1)} copy-done((f32[1,1,1024,256]{3,2,1,0:T(8,128)S(1)}, f32[1,1,1024,256]{3,2,1,0:T(8,128)}, u32[]{:S(2)}) %copy-start.2) | copy-done | bytes 1048600
  5.1 0.0 copy-start.3
  5.1 0.7 copy-done.3
  5.8 0.0 copy-start.4
  5.8 0.7 copy-done.4
  6.5 106.6 %shard_map.82 = f32[1,1,1024,256]{3,2,1,0:T(8,128)S(1)} custom-call(f32[1,1,1024,256]{3,2,1,0:T(8,128)S(1)} %copy-done.1, f32[1,1,1024,256]{3,2,1,0:T(8,128)S(1)} %copy-done.2, bf16[1,1,1024,1024]{3,2,1,0:T(8,128)(2,1)S(1)} %copy-done, bf16[1,1,1024,1024]{3,2,1,0:T(8,128)(2,1)} %pre_h.1, bf16[1,1,1024,64]{3,2,1,0:T(8,128)(2,1)S(1)} %copy.9.basis_h, ...), custom_call_target="tpu_custom_call" | custom-call | tf_op jit(solution)/shard_map/pallas_call | solution.py:328
  113.1 1.0 copy.11
Async XLA Ops:
  1.1 1.6 %copy-start = (bf16[1,1,1024,1024]{3,2,1,0:T(8,128)(2,1)S(1)}, bf16[1,1,1024,1024]{3,2,1,0:T(8,128)(2,1)}, u32[]{:S(2)}) copy-start(bf16[1,1,1024,1024]{3,2,1,0:T(8,128)(2,1)} %op_h.1) | copy-start | bytes 6291460
  2.7 1.2 %copy-start.1 = (f32[1,1,1024,256]{3,2,1,0:T(8,128)S(1)}, f32[1,1,1024,256]{3,2,1,0:T(8,128)}, u32[]{:S(2)}) copy-start(f32[1,1,1024,256]{3,2,1,0:T(8,128)} %load_h.1) | copy-start | bytes 3145732
  3.9 1.2 %copy-start.2 = (f32[1,1,1024,256]{3,2,1,0:T(8,128)S(1)}, f32[1,1,1024,256]{3,2,1,0:T(8,128)}, u32[]{:S(2)}) copy-start(f32[1,1,1024,256]{3,2,1,0:T(8,128)} %guess_h.1) | copy-start | bytes 3145732
  5.1 0.7 copy-start.3
  5.8 0.7 copy-start.4

commit v2 on v1

v2 whole, which is shorter than its diff:
```python
import jax
import jax.numpy as jnp
from jax import lax
from jax.experimental import pallas as pl
from jax.experimental.pallas import tpu as pltpu
from jax.sharding import PartitionSpec as P

ITERS = 2
OMEGA = 0.6
MESH = pl.DeviceIdType.MESH
BF = jnp.bfloat16
F32 = jnp.float32
TILE = 256


def mm(left, right):
    return jnp.dot(left, right, preferred_element_type=F32)


def kernel(
    load_h, guess_h, op_h, pre_h, basis_h, coarse_h, rows_h, slot_h, out_h,
    u, load, amat, mmat, cmat, basis, rows, slot,
    pick, place, b2, b2t, keep, ub, applied, resid, fix,
    esend, erecv, cres, gath, ypart, yown, xrecv, zpart, zrecv,
    in_sem, out_sem, e_ss, e_rs, t_ss, t_rs, y_ss, y_rs, p_ss, p_rs, x_ss, x_rs, z_ss, z_rs,
):
    core = lax.axis_index("grp")
    row = lax.axis_index("row")
    col = lax.axis_index("col")
    y, zl = row // 2, lax.rem(row, 2)
    x, zh = col // 4, lax.rem(col, 4)
    a = core * 8 + row
    n_basis = basis.shape[0]

    def at_row(r, c):
        return {"grp": r // 8, "row": lax.rem(r, 8), "col": c}

    loads = [
        pltpu.make_async_copy(src, dst, in_sem.at[i])
        for i, (src, dst) in enumerate(
            [
                (rows_h.at[0], rows),
                (guess_h.at[0, 0], u),
                (op_h.at[0, 0], amat),
                (load_h.at[0, 0], load),
                (slot_h.at[0], slot),
                (basis_h, basis),
                (pre_h.at[0, 0], mmat),
                (coarse_h, cmat),
            ]
        )
    ]
    for c in loads:
        c.start()
    l_rows, l_u, l_a, l_load, l_slot, l_basis, l_m, l_c = loads

    present = [col > 0, col < 15, a > 0, a < 15]
    across = [at_row(a, col - 1), at_row(a, col + 1), at_row(a - 1, col), at_row(a + 1, col)]
    stays = [jnp.logical_and(a == col, zl == j) for j in range(2)]
    mirror = [at_row(col // 2 * 2 + j, a) for j in range(2)]
    y_peer = [{"grp": core, "row": lax.rem(y + d, 4) * 2 + zl, "col": col} for d in (1, 2, 3)]
    c_pair = {"grp": 1 - core, "row": row, "col": col}
    x_peer = [{"grp": core, "row": row, "col": lax.rem(x + d, 4) * 4 + zh} for d in (1, 2, 3)]
    h_peer = [{"grp": core, "row": row, "col": x * 4 + lax.rem(zh + d, 4)} for d in (1, 2, 3)]

    barrier = pltpu.get_barrier_semaphore()
    fixed = y_peer + [c_pair] + x_peer + h_peer
    leaves = [jnp.logical_not(p) for p in stays]
    source = [at_row(col, a // 2 * 2 + j) for j in range(2)]
    for peer in fixed:
        pl.semaphore_signal(barrier, inc=1, device_id=peer, device_id_type=MESH)
    for ok, peer in zip(present + leaves, across + source):
        @pl.when(ok)
        def _():
            pl.semaphore_signal(barrier, inc=1, device_id=peer, device_id_type=MESH)

    for k in range(4):
        @pl.when(jnp.logical_not(present[k]))
        def _():
            for e in range(2 * ITERS):
                erecv[e, k] = jnp.zeros(erecv.shape[2:], BF)

    l_rows.wait()
    ni = pick.shape[0]

    @pl.loop(0, ni // 128)
    def _(t):
        base = pl.multiple_of(t * 128, 128)
        here = rows[:, pl.ds(base, 128)].astype(F32)
        down = jnp.broadcast_to(here, (128, 128)).T.astype(jnp.int32)
        lane = lax.broadcasted_iota(jnp.int32, (128, 128), 1)
        for v in range(ni // 128):
            pick[pl.ds(base, 128), v * 128:(v + 1) * 128] = jnp.where(
                down == lane + v * 128, 1.0, 0.0
            ).astype(BF)
        sub = lax.broadcasted_iota(jnp.int32, (128, ni), 0) + base
        place[pl.ds(base, 128), :] = jnp.where(sub == rows[...], 1.0, 0.0).astype(BF)

    def tiles(body):
        for t in range(ni // TILE):
            body(pl.ds(t * TILE, TILE))

    l_u.wait()
    ub[...] = u[...].astype(BF)

    l_a.wait()

    total = len(fixed) + sum(p.astype(jnp.int32) for p in present + leaves)
    pl.semaphore_wait(barrier, total)

    def edge_copy(e, k):
        return pltpu.make_async_remote_copy(
            src_ref=esend.at[e, k], dst_ref=erecv.at[e, k ^ 1],
            send_sem=e_ss.at[e, k], recv_sem=e_rs.at[e, k ^ 1],
            device_id=across[k], device_id_type=MESH,
        )

    def edge_arrival(e, k):
        return pltpu.make_async_remote_copy(
            src_ref=esend.at[e, k], dst_ref=erecv.at[e, k],
            send_sem=e_ss.at[e, k], recv_sem=e_rs.at[e, k],
            device_id=across[k], device_id_type=MESH,
        )

    def send_edges(e, source):
        for k in (0, 1, 2, 3):
            esend[e, k] = mm(pick[k * TILE:(k + 1) * TILE, :], source).astype(BF)

            @pl.when(present[k])
            def _():
                edge_copy(e, k).start()

    def take_edges(e):
        for k in range(4):
            @pl.when(present[k])
            def _():
                edge_arrival(e, k).wait_recv()

    def beside(e):
        return erecv[e].reshape(ni, erecv.shape[3])

    def prepare():
        flag = jnp.concatenate(
            [jnp.full((TILE, 128), p.astype(F32)) for p in present], axis=0
        ).astype(BF)

        def keep_tile(at):
            keep[at, :] = 1.0 - 0.5 * mm(place[at, :], flag)

        tiles(keep_tile)

        l_slot.wait()
        l_basis.wait()
        order = (lax.broadcasted_iota(jnp.int32, (n_basis, n_basis), 0) == slot[...])
        order = jnp.where(order, 1.0, 0.0).astype(BF)
        ordered = mm(order, basis[...])
        b2t[...] = ordered.astype(BF)
        b2[...] = ordered.T.astype(BF)

    for s in range(ITERS):
        e1, e2 = 2 * s, 2 * s + 1

        def apply_tile(at):
            value = mm(amat[at, :], ub[...])
            applied[at, :] = value
            resid[at, :] = value.astype(BF)

        tiles(apply_tile)
        send_edges(e1, resid[...])
        if s == 0:
            prepare()
            l_load.wait()
        take_edges(e1)

        def resid_tile(at):
            value = load[at, :] - applied[at, :] - mm(place[at, :], beside(e1))
            resid[at, :] = value.astype(BF)

        tiles(resid_tile)

        cres[s] = mm(b2t[...], resid[...]).astype(BF)
        slot_of = gath.at[s, col // 8, lax.rem(col, 8) // 2, lax.rem(col, 2)]
        crossings = [
            pltpu.make_async_remote_copy(
                src_ref=cres.at[s], dst_ref=slot_of,
                send_sem=t_ss.at[s, j], recv_sem=t_rs.at[s, lax.rem(col, 2)],
                device_id=mirror[j], device_id_type=MESH,
            )
            for j in range(2)
        ]
        arrivals = [
            pltpu.make_async_remote_copy(
                src_ref=cres.at[s], dst_ref=gath.at[s, core, y, j],
                send_sem=t_ss.at[s, j], recv_sem=t_rs.at[s, j],
                device_id=source[j], device_id_type=MESH,
            )
            for j in range(2)
        ]
        for j in range(2):
            @pl.when(leaves[j])
            def _():
                crossings[j].start()

            @pl.when(stays[j])
            def _():
                gath[s, core, y, j] = cres[s]

        if s == 0:
            l_m.wait()

        def fix_tile(at):
            value = mm(mmat[at, :], resid[...])
            fix[at, :] = value
            applied[at, :] = value

        tiles(fix_tile)

        for j in range(2):
            @pl.when(leaves[j])
            def _():
                arrivals[j].wait_recv()

        def gather_copy(i, from_y, sems, peer):
            ref = gath.at[s, core, from_y]
            return pltpu.make_async_remote_copy(
                src_ref=ref, dst_ref=ref,
                send_sem=sems[0].at[s, i], recv_sem=sems[1].at[s, i],
                device_id=peer, device_id_type=MESH,
            )

        y_sems, p_sems = (y_ss, y_rs), (p_ss, p_rs)
        y_copies = [gather_copy(d, y, y_sems, y_peer[d]) for d in range(3)]
        for c in y_copies:
            c.start()
        p_copies = [gather_copy(3, y, p_sems, c_pair)]
        p_copies[0].start()

        ub[...] = fix[...].astype(BF)
        send_edges(e2, ub[...])

        for d in (0, 2, 1):
            from_y = lax.rem(y + 3 - d, 4)
            gather_copy(d, from_y, y_sems, y_peer[d]).wait_recv()
            c = gather_copy(d, from_y, p_sems, c_pair)
            c.start()
            p_copies.append(c)
        for d, c in zip((3, 0, 2, 1), p_copies):
            at_y = y if d == 3 else lax.rem(y + 3 - d, 4)
            other = gath.at[s, 1 - core, at_y]
            pltpu.make_async_remote_copy(
                src_ref=other, dst_ref=other,
                send_sem=p_ss.at[s, d], recv_sem=p_rs.at[s, d],
                device_id=c_pair, device_id_type=MESH,
            ).wait_recv()
        if s == 0:
            l_c.wait()
        vec = gath[s].reshape(ni, gath.shape[5])

        def block_of(d):
            to = lax.rem(x + d, 4)
            return mm(cmat[pl.ds(pl.multiple_of(to * TILE, TILE), TILE), :], vec)

        for d in range(3):
            ypart[s, d] = block_of(d + 1).astype(BF).reshape(ypart.shape[2:])

        def x_copy(j, d):
            at_h = lax.rem(zh + (2, 1, 3, 0)[j], 4)
            return pltpu.make_async_remote_copy(
                src_ref=ypart.at[s, d, at_h], dst_ref=xrecv.at[s, d, at_h],
                send_sem=x_ss.at[s, d, j], recv_sem=x_rs.at[s, d, j],
                device_id=x_peer[d], device_id_type=MESH,
            )

        x_copies = [x_copy(j, d) for j in range(4) for d in (1, 0, 2)]
        for c in x_copies:
            c.start()
        yown[...] = block_of(0).reshape(yown.shape)
        h_copies = []
        for j in range(4):
            dz = (2, 1, 3, 0)[j]
            at_h = lax.rem(zh + dz, 4)
            for c in x_copies[3 * j:3 * j + 3]:
                c.wait_recv()
            part = yown[at_h]
            for d in range(3):
                part = part + xrecv[s, d, at_h].astype(F32)
            if dz == 0:
                sol = part
                continue
            zpart[s, dz - 1] = part.astype(BF)
            c = pltpu.make_async_remote_copy(
                src_ref=zpart.at[s, dz - 1], dst_ref=zrecv.at[s, dz - 1],
                send_sem=z_ss.at[s, dz - 1], recv_sem=z_rs.at[s, dz - 1],
                device_id=h_peer[dz - 1], device_id_type=MESH,
            )
            c.start()
            h_copies.append(c)
        take_edges(e2)

        def smooth_tile(at):
            weight = jnp.concatenate([keep[at, :]] * 2, axis=1)
            fix[at, :] = weight * fix[at, :] + 0.5 * mm(place[at, :], beside(e2))

        tiles(smooth_tile)
        for c in h_copies:
            c.wait_recv()
        for d in range(3):
            sol = sol + zrecv[s, d].astype(F32)
        sol = sol.astype(BF)

        def update_tile(at):
            value = u[at, :] + OMEGA * (fix[at, :] + mm(b2[at, :], sol))
            u[at, :] = value
            ub[at, :] = value.astype(BF)

        tiles(update_tile)

        for j in range(2):
            @pl.when(leaves[j])
            def _():
                crossings[j].wait_send()
        for c in y_copies + p_copies + x_copies + h_copies:
            c.wait_send()
        for e in (e1, e2):
            for k in range(4):
                @pl.when(present[k])
                def _():
                    edge_copy(e, k).wait_send()

    done = pltpu.make_async_copy(u, out_h.at[0, 0], out_sem)
    done.start()
    done.wait()


def body(load, guess, interface_op, precond, basis, coarse_inverse, edge_rows, coarse_slot):
    ni, cases = load.shape[2:]
    nb = basis.shape[3]
    dma = pltpu.SemaphoreType.DMA
    vm = pltpu.VMEM
    anywhere = pl.BlockSpec(memory_space=pltpu.HBM)
    return pl.pallas_call(
        kernel,
        out_shape=jax.ShapeDtypeStruct(load.shape, F32),
        in_specs=[anywhere] * 8,
        out_specs=anywhere,
        scratch_shapes=[
            vm((ni, cases), F32), vm((ni, cases), F32),
            vm((ni, ni), BF), vm((ni, ni), BF), vm((ni, ni), BF),
            vm((nb, ni), BF), vm((1, ni), jnp.int32), vm((1, nb), jnp.int32),
            vm((ni, ni), BF), vm((ni, ni), BF), vm((ni, nb), BF), vm((nb, ni), BF),
            vm((ni, 128), F32), vm((ni, cases), BF), vm((ni, cases), F32),
            vm((ni, cases), BF), vm((ni, cases), F32),
            vm((2 * ITERS, 4, ni // 4, cases), BF), vm((2 * ITERS, 4, ni // 4, cases), BF),
            vm((ITERS, nb, cases), BF), vm((ITERS, 2, 4, 2, nb, cases), BF),
            vm((ITERS, 3, 4, nb, cases), BF), vm((4, nb, cases), F32),
            vm((ITERS, 3, 4, nb, cases), BF),
            vm((ITERS, 3, nb, cases), BF), vm((ITERS, 3, nb, cases), BF),
            dma((8,)), dma,
            dma((2 * ITERS, 4)), dma((2 * ITERS, 4)),
            dma((ITERS, 2)), dma((ITERS, 2)),
            dma((ITERS, 3)), dma((ITERS, 3)),
            dma((ITERS, 4)), dma((ITERS, 4)),
            dma((ITERS, 3, 4)), dma((ITERS, 3, 4)),
            dma((ITERS, 3)), dma((ITERS, 3)),
        ],
        compiler_params=pltpu.CompilerParams(
            collective_id=0, has_side_effects=True, vmem_limit_bytes=60 * 1024 * 1024
        ),
    )(load, guess, interface_op, precond, basis[0, 0].T, coarse_inverse, edge_rows, coarse_slot)


def solution(mesh):
    cells = (("grp", "row"), "col")
    return jax.shard_map(
        body,
        mesh=mesh,
        in_specs=(
            P(*cells, None, None),
            P(*cells, None, None),
            P(*cells, None, None),
            P(*cells, None, None),
            P(*cells, None, None),
            P(*cells),
            P(*cells, None),
            P(*cells, None),
        ),
        out_specs=P(*cells, None, None),
        check_vma=False,
    )
```

time: 115 us -> 92.1 us (0.80)
  Pallas kernels: 107 us -> 89.7 us
  local copies, waits for them, and re-layouts: 7.42 us -> 2.26 us
    pallas_call x1, Pallas kernels: 107 us -> 89.7 us  [body(): pl.pallas_call(kernel, out_shape=jax.ShapeDtypeStruct(load.shape, F32), i...]
    unnamed x12 -> x1, local copies, waits for them, and re-layouts: 7.42 us -> 2.26 us
where the time goes in v2:
time: 92.1 us; the launch traced here: 92 us
  Pallas kernels  89.7 us (97%)
  local copies, waits for them, and re-layouts  2.26 us (2%)
    pallas_call x1, Pallas kernels, body(): pl.pallas_call(kernel, out_shape=jax.ShapeDtypeStruct(load.shape, F32), i...  89.7 us
    unnamed x1, local copies, waits for them, and re-layouts  2.26 us

profile of v2, /device:TPU:1, one launch (start us, length us, event | category | flops | bytes accessed | tf_op | source)
XLA Modules:
  0.0 92.0 jit_solution(6838018031682053847)
XLA Ops:
  0.0 89.7 %shard_map.82 = f32[1,1,1024,256]{3,2,1,0:T(8,128)} custom-call(f32[1,1,1024,256]{3,2,1,0:T(8,128)} %load_h.1, f32[1,1,1024,256]{3,2,1,0:T(8,128)} %guess_h.1, bf16[1,1,1024,1024]{3,2,1,0:T(8,128)(2,1)} %op_h.1, bf16[1,1,1024,1024]{3,2,1,0:T(8,128)(2,1)} %pre_h.1, bf16[64,1024]{1,0:T(8,128)(2,1)} %bitcast.3, bf16[1024,1024]{1,0:T(8,128)(2,1)} %coarse_h.1, ...), custom_call_target="tpu_custom_call" | custom-call | tf_op jit(solution)/shard_map/pallas_call | solution.py:341
  89.7 2.3 %copy.10 = f32[1,1,1024,256]{3,2,1,0:T(8,128)} copy(f32[1,1,1024,256]{3,2,1,0:T(8,128)} %shard_map.82) | data formatting | bytes 2097152

commit v3 on v2

--- a/solution.py
+++ b/solution.py
@@ -21,8 +21,8 @@
     load_h, guess_h, op_h, pre_h, basis_h, coarse_h, rows_h, slot_h, out_h,
     u, load, amat, mmat, cmat, basis, rows, slot,
     pick, place, b2, b2t, keep, ub, applied, resid, fix,
-    esend, erecv, cres, gath, ypart, yown, xrecv, zpart, zrecv,
-    in_sem, out_sem, e_ss, e_rs, t_ss, t_rs, y_ss, y_rs, p_ss, p_rs, x_ss, x_rs, z_ss, z_rs,
+    esend, erecv, bedge, bnear, csend, crecv, cres, gath, ypart, yown, xrecv, zpart, zrecv,
+    in_sem, out_sem, e_ss, e_rs, n_ss, n_rs, q_ss, q_rs, t_ss, t_rs, y_ss, y_rs, p_ss, p_rs, x_ss, x_rs, z_ss, z_rs,
 ):
     core = lax.axis_index("grp")
     row = lax.axis_index("row")
@@ -40,11 +40,11 @@
         for i, (src, dst) in enumerate(
             [
                 (rows_h.at[0], rows),
+                (slot_h.at[0], slot),
+                (basis_h, basis),
                 (guess_h.at[0, 0], u),
                 (op_h.at[0, 0], amat),
                 (load_h.at[0, 0], load),
-                (slot_h.at[0], slot),
-                (basis_h, basis),
                 (pre_h.at[0, 0], mmat),
                 (coarse_h, cmat),
             ]
@@ -52,7 +52,7 @@
     ]
     for c in loads:
         c.start()
-    l_rows, l_u, l_a, l_load, l_slot, l_basis, l_m, l_c = loads
+    l_rows, l_slot, l_basis, l_u, l_a, l_load, l_m, l_c = loads
 
     present = [col > 0, col < 15, a > 0, a < 15]
     across = [at_row(a, col - 1), at_row(a, col + 1), at_row(a - 1, col), at_row(a + 1, col)]
@@ -79,6 +79,8 @@
         def _():
             for e in range(2 * ITERS):
                 erecv[e, k] = jnp.zeros(erecv.shape[2:], BF)
+            for s in range(ITERS):
+                crecv[s, k] = jnp.zeros(crecv.shape[2:], BF)
 
     l_rows.wait()
     ni = pick.shape[0]
@@ -100,10 +102,16 @@
         for t in range(ni // TILE):
             body(pl.ds(t * TILE, TILE))
 
-    l_u.wait()
-    ub[...] = u[...].astype(BF)
-
-    l_a.wait()
+    l_slot.wait()
+    l_basis.wait()
+    order = (lax.broadcasted_iota(jnp.int32, (n_basis, n_basis), 0) == slot[...])
+    order = jnp.where(order, 1.0, 0.0).astype(BF)
+    ordered = mm(order, basis[...])
+    b2t[...] = ordered.astype(BF)
+    b2[...] = ordered.T.astype(BF)
+    for k in range(4):
+        bedge[k] = mm(b2t[...], place[:, k * TILE:(k + 1) * TILE]).astype(BF)
+
 
     total = len(fixed) + sum(p.astype(jnp.int32) for p in present + leaves)
     pl.semaphore_wait(barrier, total)
@@ -122,13 +130,27 @@
             device_id=across[k], device_id_type=MESH,
         )
 
-    def send_edges(e, source):
-        for k in (0, 1, 2, 3):
-            esend[e, k] = mm(pick[k * TILE:(k + 1) * TILE, :], source).astype(BF)
-
-            @pl.when(present[k])
-            def _():
-                edge_copy(e, k).start()
+    def select_edge(e, k, source):
+        esend[e, k] = mm(pick[k * TILE:(k + 1) * TILE, :], source).astype(BF)
+
+    def start_edge(e, k):
+        @pl.when(present[k])
+        def _():
+            edge_copy(e, k).start()
+
+    def basis_copy(k, to):
+        return pltpu.make_async_remote_copy(
+            src_ref=bedge.at[k], dst_ref=bnear.at[to],
+            send_sem=n_ss.at[k], recv_sem=n_rs.at[to],
+            device_id=across[k], device_id_type=MESH,
+        )
+
+    def product_copy(s, k, to):
+        return pltpu.make_async_remote_copy(
+            src_ref=csend.at[s, k], dst_ref=crecv.at[s, to],
+            send_sem=q_ss.at[s, k], recv_sem=q_rs.at[s, to],
+            device_id=across[k], device_id_type=MESH,
+        )
 
     def take_edges(e):
         for k in range(4):
@@ -149,13 +171,14 @@
 
         tiles(keep_tile)
 
-        l_slot.wait()
-        l_basis.wait()
-        order = (lax.broadcasted_iota(jnp.int32, (n_basis, n_basis), 0) == slot[...])
-        order = jnp.where(order, 1.0, 0.0).astype(BF)
-        ordered = mm(order, basis[...])
-        b2t[...] = ordered.astype(BF)
-        b2[...] = ordered.T.astype(BF)
+    for k in range(4):
+        @pl.when(present[k])
+        def _():
+            basis_copy(k, k ^ 1).start()
+
+    l_u.wait()
+    ub[...] = u[...].astype(BF)
+    l_a.wait()
 
     for s in range(ITERS):
         e1, e2 = 2 * s, 2 * s + 1
@@ -166,19 +189,35 @@
             resid[at, :] = value.astype(BF)
 
         tiles(apply_tile)
-        send_edges(e1, resid[...])
+        for k in range(4):
+            select_edge(e1, k, resid[...])
         if s == 0:
             prepare()
+        for k in range(4):
+            @pl.when(present[k])
+            def _():
+                if s == 0:
+                    basis_copy(k, k).wait_recv()
+                csend[s, k] = mm(bnear[k], esend[e1, k]).astype(BF)
+                product_copy(s, k, k ^ 1).start()
+        for k in range(4):
+            start_edge(e1, k)
+        if s == 0:
             l_load.wait()
-        take_edges(e1)
-
-        def resid_tile(at):
-            value = load[at, :] - applied[at, :] - mm(place[at, :], beside(e1))
-            resid[at, :] = value.astype(BF)
-
-        tiles(resid_tile)
-
-        cres[s] = mm(b2t[...], resid[...]).astype(BF)
+
+        def own_tile(at):
+            resid[at, :] = (load[at, :] - applied[at, :]).astype(BF)
+
+        tiles(own_tile)
+
+        part = mm(b2t[...], resid[...])
+        for k in range(4):
+            @pl.when(present[k])
+            def _():
+                product_copy(s, k, k).wait_recv()
+        for k in range(4):
+            part = part - crecv[s, k].astype(F32)
+        cres[s] = part.astype(BF)
         slot_of = gath.at[s, col // 8, lax.rem(col, 8) // 2, lax.rem(col, 2)]
         crossings = [
             pltpu.make_async_remote_copy(
@@ -205,16 +244,6 @@
             def _():
                 gath[s, core, y, j] = cres[s]
 
-        if s == 0:
-            l_m.wait()
-
-        def fix_tile(at):
-            value = mm(mmat[at, :], resid[...])
-            fix[at, :] = value
-            applied[at, :] = value
-
-        tiles(fix_tile)
-
         for j in range(2):
             @pl.when(leaves[j])
             def _():
@@ -235,16 +264,34 @@
         p_copies = [gather_copy(3, y, p_sems, c_pair)]
         p_copies[0].start()
 
-        ub[...] = fix[...].astype(BF)
-        send_edges(e2, ub[...])
-
         for d in (0, 2, 1):
             from_y = lax.rem(y + 3 - d, 4)
             gather_copy(d, from_y, y_sems, y_peer[d]).wait_recv()
             c = gather_copy(d, from_y, p_sems, c_pair)
             c.start()
             p_copies.append(c)
-        for d, c in zip((3, 0, 2, 1), p_copies):
+
+        take_edges(e1)
+
+        def resid_tile(at):
+            value = load[at, :] - applied[at, :] - mm(place[at, :], beside(e1))
+            resid[at, :] = value.astype(BF)
+
+        tiles(resid_tile)
+        if s == 0:
+            l_m.wait()
+
+        def fix_tile(at):
+            value = mm(mmat[at, :], resid[...])
+            fix[at, :] = value
+            ub[at, :] = value.astype(BF)
+
+        tiles(fix_tile)
+        for k in range(4):
+            select_edge(e2, k, ub[...])
+            start_edge(e2, k)
+
+        for d in (3, 0, 2, 1):
             at_y = y if d == 3 else lax.rem(y + 3 - d, 4)
             other = gath.at[s, 1 - core, at_y]
             pltpu.make_async_remote_copy(
@@ -321,11 +368,14 @@
                 crossings[j].wait_send()
         for c in y_copies + p_copies + x_copies + h_copies:
             c.wait_send()
-        for e in (e1, e2):
-            for k in range(4):
-                @pl.when(present[k])
-                def _():
-                    edge_copy(e, k).wait_send()
+        for k in range(4):
+            @pl.when(present[k])
+            def _():
+                edge_copy(e1, k).wait_send()
+                edge_copy(e2, k).wait_send()
+                product_copy(s, k, k ^ 1).wait_send()
+                if s == 0:
+                    basis_copy(k, k ^ 1).wait_send()
 
     done = pltpu.make_async_copy(u, out_h.at[0, 0], out_sem)
     done.start()
@@ -351,12 +401,16 @@
             vm((ni, 128), F32), vm((ni, cases), BF), vm((ni, cases), F32),
             vm((ni, cases), BF), vm((ni, cases), F32),
             vm((2 * ITERS, 4, ni // 4, cases), BF), vm((2 * ITERS, 4, ni // 4, cases), BF),
+            vm((4, nb, ni // 4), BF), vm((4, nb, ni // 4), BF),
+            vm((ITERS, 4, nb, cases), BF), vm((ITERS, 4, nb, cases), BF),
             vm((ITERS, nb, cases), BF), vm((ITERS, 2, 4, 2, nb, cases), BF),
             vm((ITERS, 3, 4, nb, cases), BF), vm((4, nb, cases), F32),
             vm((ITERS, 3, 4, nb, cases), BF),
             vm((ITERS, 3, nb, cases), BF), vm((ITERS, 3, nb, cases), BF),
             dma((8,)), dma,
             dma((2 * ITERS, 4)), dma((2 * ITERS, 4)),
+            dma((4,)), dma((4,)),
+            dma((ITERS, 4)), dma((ITERS, 4)),
             dma((ITERS, 2)), dma((ITERS, 2)),
             dma((ITERS, 3)), dma((ITERS, 3)),
             dma((ITERS, 4)), dma((ITERS, 4)),

time: 92.1 us -> 104 us (1.13)
  the two profiles are of different devices: /device:TPU:1 before, /device:TPU:16 now
where the time goes in v3:
time: 104 us
  Pallas kernels  102 us (98%)
  local copies, waits for them, and re-layouts  2.26 us (2%)
    pallas_call x1, Pallas kernels, body(): pl.pallas_call(kernel, out_shape=jax.ShapeDtypeStruct(load.shape, F32), i...  102 us
    unnamed x1, local copies, waits for them, and re-layouts  2.26 us

profile of v3, /device:TPU:16, one launch (start us, length us, event | category | flops | bytes accessed | tf_op | source)
XLA Modules:
  0.0 103.8 jit_solution(8966822441717437577)
XLA Ops:
  0.0 101.5 %shard_map.82 = f32[1,1,1024,256]{3,2,1,0:T(8,128)} custom-call(f32[1,1,1024,256]{3,2,1,0:T(8,128)} %load_h.1, f32[1,1,1024,256]{3,2,1,0:T(8,128)} %guess_h.1, bf16[1,1,1024,1024]{3,2,1,0:T(8,128)(2,1)} %op_h.1, bf16[1,1,1024,1024]{3,2,1,0:T(8,128)(2,1)} %pre_h.1, bf16[64,1024]{1,0:T(8,128)(2,1)} %bitcast.3, bf16[1024,1024]{1,0:T(8,128)(2,1)} %coarse_h.1, ...), custom_call_target="tpu_custom_call" | custom-call | tf_op jit(solution)/shard_map/pallas_call | solution.py:391
  101.5 2.3 %copy.10 = f32[1,1,1024,256]{3,2,1,0:T(8,128)} copy(f32[1,1,1024,256]{3,2,1,0:T(8,128)} %shard_map.82) | data formatting | bytes 2097152

commit v4 on v2

--- a/solution.py
+++ b/solution.py
@@ -21,7 +21,7 @@
     load_h, guess_h, op_h, pre_h, basis_h, coarse_h, rows_h, slot_h, out_h,
     u, load, amat, mmat, cmat, basis, rows, slot,
     pick, place, b2, b2t, keep, ub, applied, resid, fix,
-    esend, erecv, cres, gath, ypart, yown, xrecv, zpart, zrecv,
+    pa, mplace, bedge, cown, esend, erecv, cres, gath, ypart, yown, xrecv, zpart, zrecv,
     in_sem, out_sem, e_ss, e_rs, t_ss, t_rs, y_ss, y_rs, p_ss, p_rs, x_ss, x_rs, z_ss, z_rs,
 ):
     core = lax.axis_index("grp")
@@ -105,9 +105,6 @@
 
     l_a.wait()
 
-    total = len(fixed) + sum(p.astype(jnp.int32) for p in present + leaves)
-    pl.semaphore_wait(barrier, total)
-
     def edge_copy(e, k):
         return pltpu.make_async_remote_copy(
             src_ref=esend.at[e, k], dst_ref=erecv.at[e, k ^ 1],
@@ -122,13 +119,16 @@
             device_id=across[k], device_id_type=MESH,
         )
 
+    def start_edge(e, k):
+        @pl.when(present[k])
+        def _():
+            edge_copy(e, k).start()
+
     def send_edges(e, source):
         for k in (0, 1, 2, 3):
             esend[e, k] = mm(pick[k * TILE:(k + 1) * TILE, :], source).astype(BF)
 
-            @pl.when(present[k])
-            def _():
-                edge_copy(e, k).start()
+            start_edge(e, k)
 
     def take_edges(e):
         for k in range(4):
@@ -156,29 +156,51 @@
         ordered = mm(order, basis[...])
         b2t[...] = ordered.astype(BF)
         b2[...] = ordered.T.astype(BF)
-
+        bedge[...] = mm(b2t[...], place[...]).astype(BF)
+        l_m.wait()
+
+        @pl.loop(0, ni // TILE)
+        def _(t):
+            at = pl.ds(pl.multiple_of(t * TILE, TILE), TILE)
+            mplace[at, :] = mm(mmat[at, :], place[...]).astype(BF)
+            pa[at, :] = mm(pick[at, :], amat[...]).astype(BF)
+
+    outs = []
     for s in range(ITERS):
         e1, e2 = 2 * s, 2 * s + 1
+
+        if s > 0:
+            for k in range(4):
+                esend[e1, k] = mm(pa[k * TILE:(k + 1) * TILE, :], ub[...]).astype(BF)
+                start_edge(e1, k)
 
         def apply_tile(at):
             value = mm(amat[at, :], ub[...])
             applied[at, :] = value
-            resid[at, :] = value.astype(BF)
+            if s == 0:
+                resid[at, :] = value.astype(BF)
 
         tiles(apply_tile)
-        send_edges(e1, resid[...])
         if s == 0:
+            total = len(fixed) + sum(p.astype(jnp.int32) for p in present + leaves)
+            pl.semaphore_wait(barrier, total)
+            send_edges(e1, resid[...])
             prepare()
             l_load.wait()
+
+        def own_tile(at):
+            resid[at, :] = (load[at, :] - applied[at, :]).astype(BF)
+
+        tiles(own_tile)
+        cown[...] = mm(b2t[...], resid[...])
+
+        def own_fix_tile(at):
+            fix[at, :] = mm(mmat[at, :], resid[...])
+
+        tiles(own_fix_tile)
         take_edges(e1)
 
-        def resid_tile(at):
-            value = load[at, :] - applied[at, :] - mm(place[at, :], beside(e1))
-            resid[at, :] = value.astype(BF)
-
-        tiles(resid_tile)
-
-        cres[s] = mm(b2t[...], resid[...]).astype(BF)
+        cres[s] = (cown[...] - mm(bedge[...], beside(e1))).astype(BF)
         slot_of = gath.at[s, col // 8, lax.rem(col, 8) // 2, lax.rem(col, 2)]
         crossings = [
             pltpu.make_async_remote_copy(
@@ -205,13 +227,10 @@
             def _():
                 gath[s, core, y, j] = cres[s]
 
-        if s == 0:
-            l_m.wait()
-
         def fix_tile(at):
-            value = mm(mmat[at, :], resid[...])
+            value = fix[at, :] - mm(mplace[at, :], beside(e1))
             fix[at, :] = value
-            applied[at, :] = value
+            ub[at, :] = value.astype(BF)
 
         tiles(fix_tile)
 
@@ -235,7 +254,6 @@
         p_copies = [gather_copy(3, y, p_sems, c_pair)]
         p_copies[0].start()
 
-        ub[...] = fix[...].astype(BF)
         send_edges(e2, ub[...])
 
         for d in (0, 2, 1):
@@ -311,7 +329,14 @@
         def update_tile(at):
             value = u[at, :] + OMEGA * (fix[at, :] + mm(b2[at, :], sol))
             u[at, :] = value
-            ub[at, :] = value.astype(BF)
+            if s < ITERS - 1:
+                ub[at, :] = value.astype(BF)
+            else:
+                c = pltpu.make_async_copy(
+                    u.at[at], out_h.at[0, 0, at], out_sem.at[len(outs)]
+                )
+                c.start()
+                outs.append(c)
 
         tiles(update_tile)
 
@@ -327,9 +352,8 @@
                 def _():
                     edge_copy(e, k).wait_send()
 
-    done = pltpu.make_async_copy(u, out_h.at[0, 0], out_sem)
-    done.start()
-    done.wait()
+    for c in outs:
+        c.wait()
 
 
 def body(load, guess, interface_op, precond, basis, coarse_inverse, edge_rows, coarse_slot):
@@ -350,12 +374,13 @@
             vm((ni, ni), BF), vm((ni, ni), BF), vm((ni, nb), BF), vm((nb, ni), BF),
             vm((ni, 128), F32), vm((ni, cases), BF), vm((ni, cases), F32),
             vm((ni, cases), BF), vm((ni, cases), F32),
+            vm((ni, ni), BF), vm((ni, ni), BF), vm((nb, ni), BF), vm((nb, cases), F32),
             vm((2 * ITERS, 4, ni // 4, cases), BF), vm((2 * ITERS, 4, ni // 4, cases), BF),
             vm((ITERS, nb, cases), BF), vm((ITERS, 2, 4, 2, nb, cases), BF),
             vm((ITERS, 3, 4, nb, cases), BF), vm((4, nb, cases), F32),
             vm((ITERS, 3, 4, nb, cases), BF),
             vm((ITERS, 3, nb, cases), BF), vm((ITERS, 3, nb, cases), BF),
-            dma((8,)), dma,
+            dma((8,)), dma((4,)),
             dma((2 * ITERS, 4)), dma((2 * ITERS, 4)),
             dma((ITERS, 2)), dma((ITERS, 2)),
             dma((ITERS, 3)), dma((ITERS, 3)),

time: 92.1 us -> 90.1 us (0.978)
  Pallas kernels: 89.7 us -> 87.2 us
    pallas_call x1, Pallas kernels: 89.7 us -> 87.2 us  [body(): pl.pallas_call(kernel, out_shape=jax.ShapeDtypeStruct(load.shape, F32), i...]
where the time goes in v4:
time: 90.1 us; the launch traced here: 89.5 us
  Pallas kernels  87.2 us (97%)
  local copies, waits for them, and re-layouts  2.26 us (3%)
    pallas_call x1, Pallas kernels, body(): pl.pallas_call(kernel, out_shape=jax.ShapeDtypeStruct(load.shape, F32), i...  87.2 us
    unnamed x1, local copies, waits for them, and re-layouts  2.26 us

profile of v4, /device:TPU:1, one launch (start us, length us, event | category | flops | bytes accessed | tf_op | source)
XLA Modules:
  0.0 89.5 jit_solution(4793408015074398865)
XLA Ops:
  0.0 87.2 %shard_map.82 = f32[1,1,1024,256]{3,2,1,0:T(8,128)} custom-call(f32[1,1,1024,256]{3,2,1,0:T(8,128)} %load_h.1, f32[1,1,1024,256]{3,2,1,0:T(8,128)} %guess_h.1, bf16[1,1,1024,1024]{3,2,1,0:T(8,128)(2,1)} %op_h.1, bf16[1,1,1024,1024]{3,2,1,0:T(8,128)(2,1)} %pre_h.1, bf16[64,1024]{1,0:T(8,128)(2,1)} %bitcast.3, bf16[1024,1024]{1,0:T(8,128)(2,1)} %coarse_h.1, ...), custom_call_target="tpu_custom_call" | custom-call | tf_op jit(solution)/shard_map/pallas_call | solution.py:365
  87.2 2.3 %copy.10 = f32[1,1,1024,256]{3,2,1,0:T(8,128)} copy(f32[1,1,1024,256]{3,2,1,0:T(8,128)} %shard_map.82) | data formatting | bytes 2097152

commit v5 on v4

--- a/solution.py
+++ b/solution.py
@@ -21,7 +21,7 @@
     load_h, guess_h, op_h, pre_h, basis_h, coarse_h, rows_h, slot_h, out_h,
     u, load, amat, mmat, cmat, basis, rows, slot,
     pick, place, b2, b2t, keep, ub, applied, resid, fix,
-    pa, mplace, bedge, cown, esend, erecv, cres, gath, ypart, yown, xrecv, zpart, zrecv,
+    pa, pab, mplace, bedge, cown, yhalf, esend, erecv, cres, gath, ypart, yown, xrecv, zpart, zrecv,
     in_sem, out_sem, e_ss, e_rs, t_ss, t_rs, y_ss, y_rs, p_ss, p_rs, x_ss, x_rs, z_ss, z_rs,
 ):
     core = lax.axis_index("grp")
@@ -161,18 +161,14 @@
 
         @pl.loop(0, ni // TILE)
         def _(t):
-            at = pl.ds(pl.multiple_of(t * TILE, TILE), TILE)
-            mplace[at, :] = mm(mmat[at, :], place[...]).astype(BF)
-            pa[at, :] = mm(pick[at, :], amat[...]).astype(BF)
+            across_at = pl.ds(pl.multiple_of(t * TILE, TILE), TILE)
+            mplace[:, across_at] = mm(mmat[...], place[:, across_at]).astype(BF)
+            pa[:, across_at] = mm(pick[...], amat[:, across_at]).astype(BF)
+        pab[...] = mm(pa[...], b2[...]).astype(BF)
 
     outs = []
     for s in range(ITERS):
         e1, e2 = 2 * s, 2 * s + 1
-
-        if s > 0:
-            for k in range(4):
-                esend[e1, k] = mm(pa[k * TILE:(k + 1) * TILE, :], ub[...]).astype(BF)
-                start_edge(e1, k)
 
         def apply_tile(at):
             value = mm(amat[at, :], ub[...])
@@ -262,6 +258,14 @@
             c = gather_copy(d, from_y, p_sems, c_pair)
             c.start()
             p_copies.append(c)
+        if s == 0:
+            l_c.wait()
+        span = ni // 2
+        own_at = pl.ds(pl.multiple_of(core * span, span), span)
+        other_at = pl.ds(pl.multiple_of((1 - core) * span, span), span)
+        ready = gath[s, core].reshape(span, gath.shape[5])
+        for k in range(4):
+            yhalf[k] = mm(cmat[k * TILE:(k + 1) * TILE, own_at], ready)
         for d, c in zip((3, 0, 2, 1), p_copies):
             at_y = y if d == 3 else lax.rem(y + 3 - d, 4)
             other = gath.at[s, 1 - core, at_y]
@@ -270,13 +274,12 @@
                 send_sem=p_ss.at[s, d], recv_sem=p_rs.at[s, d],
                 device_id=c_pair, device_id_type=MESH,
             ).wait_recv()
-        if s == 0:
-            l_c.wait()
-        vec = gath[s].reshape(ni, gath.shape[5])
+        vec = gath[s, 1 - core].reshape(span, gath.shape[5])
 
         def block_of(d):
             to = lax.rem(x + d, 4)
-            return mm(cmat[pl.ds(pl.multiple_of(to * TILE, TILE), TILE), :], vec)
+            at = pl.ds(pl.multiple_of(to * TILE, TILE), TILE)
+            return yhalf[to] + mm(cmat[at, other_at], vec)
 
         for d in range(3):
             ypart[s, d] = block_of(d + 1).astype(BF).reshape(ypart.shape[2:])
@@ -320,11 +323,27 @@
             fix[at, :] = weight * fix[at, :] + 0.5 * mm(place[at, :], beside(e2))
 
         tiles(smooth_tile)
+        if s < ITERS - 1:
+            def ahead_tile(at):
+                ub[at, :] = (u[at, :] + OMEGA * fix[at, :]).astype(BF)
+
+            def ahead_edge(at):
+                applied[at, :] = mm(pa[at, :], ub[...])
+
+            tiles(ahead_tile)
+            tiles(ahead_edge)
         for c in h_copies:
             c.wait_recv()
         for d in range(3):
             sol = sol + zrecv[s, d].astype(F32)
         sol = sol.astype(BF)
+
+        if s < ITERS - 1:
+            for k in range(4):
+                at = slice(k * TILE, (k + 1) * TILE)
+                value = applied[at, :] + OMEGA * mm(pab[at, :], sol)
+                esend[e1 + 2, k] = value.astype(BF)
+                start_edge(e1 + 2, k)
 
         def update_tile(at):
             value = u[at, :] + OMEGA * (fix[at, :] + mm(b2[at, :], sol))
@@ -374,7 +393,8 @@
             vm((ni, ni), BF), vm((ni, ni), BF), vm((ni, nb), BF), vm((nb, ni), BF),
             vm((ni, 128), F32), vm((ni, cases), BF), vm((ni, cases), F32),
             vm((ni, cases), BF), vm((ni, cases), F32),
-            vm((ni, ni), BF), vm((ni, ni), BF), vm((nb, ni), BF), vm((nb, cases), F32),
+            vm((ni, ni), BF), vm((ni, nb), BF), vm((ni, ni), BF), vm((nb, ni), BF), vm((nb, cases), F32),
+            vm((4, TILE, cases), F32),
             vm((2 * ITERS, 4, ni // 4, cases), BF), vm((2 * ITERS, 4, ni // 4, cases), BF),
             vm((ITERS, nb, cases), BF), vm((ITERS, 2, 4, 2, nb, cases), BF),
             vm((ITERS, 3, 4, nb, cases), BF), vm((4, nb, cases), F32),

time: 90.1 us -> 89 us (0.988)
  Pallas kernels: 87.2 us -> 85.7 us
    pallas_call x1, Pallas kernels: 87.2 us -> 85.7 us  [body(): pl.pallas_call(kernel, out_shape=jax.ShapeDtypeStruct(load.shape, F32), i...]
where the time goes in v5:
time: 89 us; the launch traced here: 88 us
  Pallas kernels  85.7 us (96%)
  local copies, waits for them, and re-layouts  2.26 us (3%)
    pallas_call x1, Pallas kernels, body(): pl.pallas_call(kernel, out_shape=jax.ShapeDtypeStruct(load.shape, F32), i...  85.7 us
    unnamed x1, local copies, waits for them, and re-layouts  2.26 us

profile of v5, /device:TPU:1, one launch (start us, length us, event | category | flops | bytes accessed | tf_op | source)
XLA Modules:
  0.0 88.0 jit_solution(9457261815279437393)
XLA Ops:
  0.0 85.7 %shard_map.82 = f32[1,1,1024,256]{3,2,1,0:T(8,128)} custom-call(f32[1,1,1024,256]{3,2,1,0:T(8,128)} %load_h.1, f32[1,1,1024,256]{3,2,1,0:T(8,128)} %guess_h.1, bf16[1,1,1024,1024]{3,2,1,0:T(8,128)(2,1)} %op_h.1, bf16[1,1,1024,1024]{3,2,1,0:T(8,128)(2,1)} %pre_h.1, bf16[64,1024]{1,0:T(8,128)(2,1)} %bitcast.3, bf16[1024,1024]{1,0:T(8,128)(2,1)} %coarse_h.1, ...), custom_call_target="tpu_custom_call" | custom-call | tf_op jit(solution)/shard_map/pallas_call | solution.py:384
  85.7 2.3 %copy.10 = f32[1,1,1024,256]{3,2,1,0:T(8,128)} copy(f32[1,1,1024,256]{3,2,1,0:T(8,128)} %shard_map.82) | data formatting | bytes 2097152

commit v6 on v5

--- a/solution.py
+++ b/solution.py
@@ -161,10 +161,10 @@
 
         @pl.loop(0, ni // TILE)
         def _(t):
-            across_at = pl.ds(pl.multiple_of(t * TILE, TILE), TILE)
-            mplace[:, across_at] = mm(mmat[...], place[:, across_at]).astype(BF)
-            pa[:, across_at] = mm(pick[...], amat[:, across_at]).astype(BF)
-        pab[...] = mm(pa[...], b2[...]).astype(BF)
+            at = pl.ds(pl.multiple_of(t * TILE, TILE), TILE)
+            mplace[at, :] = mm(mmat[at, :], place[...]).astype(BF)
+            pa[at, :] = mm(pick[at, :], amat[...]).astype(BF)
+            pab[at, :] = mm(pa[at, :], b2[...]).astype(BF)
 
     outs = []
     for s in range(ITERS):

time: 89 us -> 88.4 us (level)
  no operation moved by 1% of the time
where the time goes in v6:
time: 88.4 us; the launch traced here: 88.2 us
  Pallas kernels  85.9 us (97%)
  local copies, waits for them, and re-layouts  2.26 us (3%)
    pallas_call x1, Pallas kernels, body(): pl.pallas_call(kernel, out_shape=jax.ShapeDtypeStruct(load.shape, F32), i...  85.9 us
    unnamed x1, local copies, waits for them, and re-layouts  2.26 us

profile of v6, /device:TPU:1, one launch (start us, length us, event | category | flops | bytes accessed | tf_op | source)
XLA Modules:
  0.0 88.2 jit_solution(10032265001480475652)
XLA Ops:
  0.0 85.9 %shard_map.82 = f32[1,1,1024,256]{3,2,1,0:T(8,128)} custom-call(f32[1,1,1024,256]{3,2,1,0:T(8,128)} %load_h.1, f32[1,1,1024,256]{3,2,1,0:T(8,128)} %guess_h.1, bf16[1,1,1024,1024]{3,2,1,0:T(8,128)(2,1)} %op_h.1, bf16[1,1,1024,1024]{3,2,1,0:T(8,128)(2,1)} %pre_h.1, bf16[64,1024]{1,0:T(8,128)(2,1)} %bitcast.3, bf16[1024,1024]{1,0:T(8,128)(2,1)} %coarse_h.1, ...), custom_call_target="tpu_custom_call" | custom-call | tf_op jit(solution)/shard_map/pallas_call | solution.py:384
  85.9 2.3 %copy.10 = f32[1,1,1024,256]{3,2,1,0:T(8,128)} copy(f32[1,1,1024,256]{3,2,1,0:T(8,128)} %shard_map.82) | data formatting | bytes 2097152
